TPU v7x, 256 devices: a whole 4x4x8 slice. The times are simulated.
256 devices in a mesh: ctx: 32 (over z, x), grp: 8 (over y, core).
Axes of the slice: x: 4, y: 4, z: 8, core: 2. Of those that a mesh axis runs over, the one named last changes fastest.
Arguments:
- queries: bfloat16 [262144, 512], P(('grp', 'ctx')), parts along dimension 0, may hold values from -6 to 6
- key_vectors: bfloat16 [262144, 512], P(('grp', 'ctx')), parts along dimension 0, may hold values from -6 to 6
- value_rows: bfloat16 [262144, 512], P(('grp', 'ctx')), parts along dimension 0, may hold values from -6 to 6
- cotangent: bfloat16 [262144, 512], P(('grp', 'ctx')), parts along dimension 0, may hold values from -6 to 6
Outputs:
- attended: bfloat16 [262144, 512], P(('grp', 'ctx')), parts along dimension 0
- grad_queries: bfloat16 [262144, 512], P(('grp', 'ctx')), parts along dimension 0
- grad_keys: bfloat16 [262144, 512], P(('grp', 'ctx')), parts along dimension 0
- grad_values: bfloat16 [262144, 512], P(('grp', 'ctx')), parts along dimension 0
There are 8 independent parts, one for each index of `grp`. A program takes and returns all parts, laid end to end along the dimension named above; each array names one. Nothing has to cross between parts.
All inputs are finite; a program needn't handle non-finite values.
Results may differ from a plain program's by a relative error of at most 0.0025.
Values sent between devices are 32-bit elements; how exact they have to be, the bound alone decides.
A program may use at most 128 MiB of HBM per device.

v0:
```python
import math

import jax
import jax.numpy as jnp
from jax import lax
from jax.sharding import PartitionSpec as P

DH = 128
HEADS = 4


def entering(value, axis, combine, identity, reverse):
    devices, position = (lax.axis_size(axis), lax.axis_index(axis))
    everything = lax.all_gather(value, axis)
    start = jnp.broadcast_to(jnp.asarray(identity, value.dtype), value.shape)

    def lap(k, before):
        at = devices - 1 - k if reverse else k
        reached = at > position if reverse else at < position
        new = combine(before, everything[at])
        return jnp.where(reached, new, before)

    return lax.fori_loop(0, devices, lap, start)


def inner_first(left, right):
    return lax.dot_general(
        left, right, (((0,), (0,)), ((), ())), preferred_element_type=jnp.float32
    )


def inner_last(left, right):
    return lax.dot_general(
        left, right, (((1,), (1,)), ((), ())), preferred_element_type=jnp.float32
    )


def split_state(state):
    upper = lax.optimization_barrier(state.astype(jnp.bfloat16))
    lower = (state - upper.astype(jnp.float32)).astype(jnp.bfloat16)
    return (upper, lower)


def block_states(queries, key_vectors, value_rows, cotangent):
    width = DH
    states = []
    grads = []
    for head_index in range(HEADS):
        cols = slice(head_index * width, (head_index + 1) * width)
        states.append(inner_first(key_vectors[:, cols], value_rows[:, cols]))
        grads.append(inner_first(queries[:, cols], cotangent[:, cols]))
    return (jnp.stack(states), jnp.stack(grads))


def block_outputs(queries, key_vectors, value_rows, cotangent, prefix_state, suffix_grad, factor):
    width = DH
    length = queries.shape[0]
    causal = lax.broadcasted_iota(jnp.int32, (length, length), 0) >= lax.broadcasted_iota(
        jnp.int32, (length, length), 1
    )
    results = ([], [], [], [])
    prefix_hi, prefix_lo = split_state(prefix_state)
    suffix_hi, suffix_lo = split_state(suffix_grad)
    for head_index in range(HEADS):
        cols = slice(head_index * width, (head_index + 1) * width)
        query_head = queries[:, cols]
        key_head = key_vectors[:, cols]
        value_head = value_rows[:, cols]
        cot_head = cotangent[:, cols]
        state_hi = prefix_hi[head_index]
        state_lo = prefix_lo[head_index]
        grad_hi = suffix_hi[head_index]
        grad_lo = suffix_lo[head_index]
        weights = jnp.where(causal, inner_last(query_head, key_head), 0.0).astype(jnp.bfloat16)
        back_weights = jnp.where(causal, inner_last(cot_head, value_head), 0.0).astype(jnp.bfloat16)
        attended = (
            jnp.dot(weights, value_head, preferred_element_type=jnp.float32)
            + jnp.dot(query_head, state_hi, preferred_element_type=jnp.float32)
            + jnp.dot(query_head, state_lo, preferred_element_type=jnp.float32)
        )
        grad_q = (
            jnp.dot(back_weights, key_head, preferred_element_type=jnp.float32)
            + inner_last(cot_head, state_hi)
            + inner_last(cot_head, state_lo)
        )
        grad_k = (
            inner_first(back_weights, query_head)
            + inner_last(value_head, grad_hi)
            + inner_last(value_head, grad_lo)
        )
        grad_v = (
            inner_first(weights, cot_head)
            + jnp.dot(key_head, grad_hi, preferred_element_type=jnp.float32)
            + jnp.dot(key_head, grad_lo, preferred_element_type=jnp.float32)
        )
        for target, source in zip(results, (attended, grad_q, grad_k, grad_v)):
            target.append((factor * source).astype(jnp.bfloat16))
    return tuple((jnp.concatenate(parts, axis=1) for parts in results))


def combine_sum(earlier, later):
    return jax.tree.map(jnp.add, earlier, later)


def on_device(queries, key_vectors, value_rows, cotangent):
    devices_ctx = lax.axis_size("ctx")
    length = queries.shape[0]
    factor = 1.0 / math.sqrt(DH * length * devices_ctx)
    states_local, grads_local = block_states(queries, key_vectors, value_rows, cotangent)
    zeros_state = jnp.zeros_like(states_local)
    prefix_state = entering(states_local, "ctx", combine_sum, zeros_state, False)
    suffix_grad = entering(grads_local, "ctx", combine_sum, zeros_state, True)
    return block_outputs(
        queries, key_vectors, value_rows, cotangent, prefix_state, suffix_grad, factor
    )


def solution(mesh):
    in_specs = (
        P(("grp", "ctx"), None),
        P(("grp", "ctx"), None),
        P(("grp", "ctx"), None),
        P(("grp", "ctx"), None),
    )
    out_specs = (
        P(("grp", "ctx"), None),
        P(("grp", "ctx"), None),
        P(("grp", "ctx"), None),
        P(("grp", "ctx"), None),
    )
    return jax.shard_map(
        on_device, mesh=mesh, in_specs=in_specs, out_specs=out_specs, check_vma=False
    )
```

profile of v0, /device:TPU:1, one launch (start us, length us, event | category | flops | bytes accessed | tf_op | source)
XLA Modules:
  0.0 275.3 jit_solution(7805637029735996975)
XLA Ops:
  7.2 1.4 convolution_bitcast_fusion.35
  8.7 1.3 convolution_bitcast_fusion.34
  10.0 1.3 convolution_bitcast_fusion.33
  11.3 1.3 convolution_bitcast_fusion.32
  22.6 1.3 fusion.76
  23.9 1.6 fusion.133
  25.6 1.3 fusion.82
  26.9 1.6 fusion.146
  29.0 1.6 fusion.109
  30.6 1.3 fusion.70
  31.9 1.6 fusion.121
  33.6 1.3 fusion.155
  34.9 1.6 fusion.150
  36.5 1.3 fusion.100
  37.8 1.6 fusion.138
  39.4 1.5 fusion.94
  40.9 1.6 fusion.126
  42.5 1.3 fusion.88
  43.8 1.6 fusion.114
  45.5 69.8 %all-gather.7.cloned.1.call-done = f32[128,128,128]{2,1,0:T(8,128)} async-done(((f32[4,128,128]{2,1,0:T(8,128)}), f32[128,128,128]{2,1,0:T(8,128)}) %all-gather.7.cloned.1.call-update) | async-done | bytes 8388624 | tf_op jit(solution)/shard_map/all_gather | solution.py:14
  115.3 34.2 %while.31 = (s32[]{:T(128)}, f32[4,128,128]{2,1,0:T(8,128)S(1)}, s32[]{:T(128)}, f32[32,4,128,128]{3,2,1,0:T(8,128)}, s32[]{:T(128)}, /*index=5*/s32[]{:T(128)}, s32[]{:T(128)}, s32[]{:T(128)}) while((s32[]{:T(128)}, f32[4,128,128]{2,1,0:T(8,128)S(1)}, s32[]{:T(128)}, f32[32,4,128,128]{3,2,1,0:T(8,128)}, s32[]{:T(128)}, ...), condition=%wide.region_3.4_spmd.clone, body=%wide.region_2.3_spmd.clone.sunk | while | flops 196616 | bytes 786595 | solution.py:23
  127.0 1.1 add_select_fusion.5
  133.4 1.1 add_select_fusion.5
  150.2 63.1 %all-gather.5.cloned.1.call-done = f32[128,128,128]{2,1,0:T(8,128)} async-done(((f32[4,128,128]{2,1,0:T(8,128)}), f32[128,128,128]{2,1,0:T(8,128)}) %all-gather.5.cloned.1.call-update) | async-done | bytes 8388624 | tf_op jit(solution)/shard_map/all_gather | solution.py:14
  213.3 34.1 %while.30 = (s32[]{:T(128)}, f32[4,128,128]{2,1,0:T(8,128)S(1)}, s32[]{:T(128)}, f32[32,4,128,128]{3,2,1,0:T(8,128)}, s32[]{:T(128)}, /*index=5*/s32[]{:T(128)}) while((s32[]{:T(128)}, f32[4,128,128]{2,1,0:T(8,128)S(1)}, s32[]{:T(128)}, f32[32,4,128,128]{3,2,1,0:T(8,128)}, s32[]{:T(128)}, /*index=5*/s32[]{:T(128)}) %tuple.83), condition=%wide.region_1.2_spmd.clone, body=%wide.region_0.1_spmd.clone.sunk | while | flops 196612 | bytes 786533 | solution.py:23
  213.3 1.1 add_select_fusion.4
  254.4 1.3 copy.12
  255.8 1.4 fusion.3
  257.5 1.3 copy.15
  258.8 1.4 fusion.23
  265.7 1.3 copy.14
  267.1 1.3 copy.13
  (182 shorter events, 87.1 us)
Async XLA Ops:
  7.2 6.3 %copy-start.6 = (bf16[1024,512]{1,0:T(8,128)(2,1)S(1)}, bf16[1024,512]{1,0:T(8,128)(2,1)}, u32[]{:S(2)}) copy-start(bf16[1024,512]{1,0:T(8,128)(2,1)} %param.10) | copy-start | bytes 3145732
  7.2 6.3 %copy-start.2 = (bf16[1024,512]{1,0:T(8,128)(2,1)S(1)}, bf16[1024,512]{1,0:T(8,128)(2,1)}, u32[]{:S(2)}) copy-start(bf16[1024,512]{1,0:T(8,128)(2,1)} %param.9) | copy-start | bytes 3145732
  7.2 108.1 %all-gather.7.cloned.1.call-start = ((), (), s32[]{:S(2)}) async-start(), calls=%async_computation.1 | async-start | bytes 8650752 | tf_op jit(solution)/shard_map/all_gather | solution.py:14
  12.6 2.7 copy-start
  13.4 199.9 %all-gather.5.cloned.1.call-start = ((), (), s32[]{:S(2)}) async-start(), calls=%async_computation | async-start | bytes 8650752 | tf_op jit(solution)/shard_map/all_gather | solution.py:14
  16.9 1.2 copy-start.3
  18.1 1.2 copy-start.1
  18.1 1.5 copy-start.7
  213.3 34.2 %copy-start.21 = (f32[1024,128]{0,1:T(8,128)S(1)}, f32[1024,128]{0,1:T(8,128)}, u32[]{:S(2)}) copy-start(f32[1024,128]{0,1:T(8,128)} %fusion.133) | copy-start | bytes 1572868
  247.4 1.3 copy-start.4
  247.4 1.4 copy-start.14
  247.4 1.7 copy-start.20
  247.5 6.4 %copy-start.22 = (bf16[4,128,128]{2,1,0:T(8,128)(2,1)}, bf16[4,128,128]{2,1,0:T(8,128)(2,1)S(1)}, u32[]{:S(2)}) copy-start(bf16[4,128,128]{2,1,0:T(8,128)(2,1)S(1)} %convert_element_type.91) | copy-start | bytes 393220
  247.5 6.6 %copy-start.25 = (bf16[4,128,128]{2,1,0:T(8,128)(2,1)}, bf16[4,128,128]{2,1,0:T(8,128)(2,1)S(1)}, u32[]{:S(2)}) copy-start(bf16[4,128,128]{2,1,0:T(8,128)(2,1)S(1)} %subtract_convert_fusion.1) | copy-start | bytes 393220
  248.9 1.1 copy-start.13
  249.1 1.1 copy-start.24
  249.6 2.5 copy-start.19
  252.1 1.7 copy-start.18
  254.3 1.4 copy-start.5
  255.8 1.6 copy-start.27
  255.8 1.6 copy-start.28
  255.8 1.6 copy-start.29
  257.4 1.4 copy-start.23
  257.5 3.7 %copy-start.8 = (bf16[1024,512]{1,0:T(8,128)(2,1)S(1)}, bf16[1024,512]{1,0:T(8,128)(2,1)}, u32[]{:S(2)}) copy-start(bf16[1024,512]{1,0:T(8,128)(2,1)} %param.10) | copy-start | bytes 3145732
  258.8 2.4 copy-start.12
  258.8 2.9 %copy-start.17 = (f32[1024,128]{0,1:T(8,128)S(1)}, f32[1024,128]{0,1:T(8,128)}, u32[]{:S(2)}) copy-start(f32[1024,128]{0,1:T(8,128)} %fusion.138) | copy-start | bytes 1572868
  261.2 1.1 copy-start.11
  261.7 1.1 copy-start.16
  262.4 1.1 copy-start.10
  262.9 1.1 copy-start.15
  263.5 1.7 copy-start.9
  265.6 1.4 copy-start.30
  (1 other events, 0.9 us)
Sparse Core Ops, SparseCore 0:
  13.5 101.6 all-gather.6
  117.8 95.4 all-gather.4
where the time goes:
time: 278 us; the launch traced here: 275 us
  waiting for transfers between devices  133 us (48%)
  other arithmetic  69.2 us (25%)
  matrix products  48.7 us (18%)
  between operations  14.8 us (5%)
  local copies, waits for them, and re-layouts  8.02 us (3%)
    all_gather x2, waiting for transfers between devices, entering(): everything = lax.all_gather(value, axis)  133 us
    select_n x64, other arithmetic, lap(): return jnp.where(reached, new, before)  66.7 us
    dot_general x16, matrix products, inner_first(): lax.dot_general(left, right, (((0,), (0,)), ((), ())), preferred_element_...  16.2 us
    dot_general x24, matrix products, inner_last(): lax.dot_general(left, right, (((1,), (1,)), ((), ())), preferred_element_...  12.3 us
    unnamed x66, local copies, waits for them, and re-layouts  8.02 us
    dot_general x4, matrix products, block_outputs(): jnp.dot(back_weights, key_head, preferred_element_type=jnp.float32)  6.51 us
    dot_general x4, matrix products, block_outputs(): jnp.dot(weights, value_head, preferred_element_type=jnp.float32)  6.49 us
  transfers between devices with their start and end apart: 2, of which 2 were waited for; matrix products, arithmetic and copies ran while one was open for 23% of the time, Pallas kernels for 0%

commit v1 on v0

v1 whole, which is shorter than its diff:
```python
import functools
import math

import jax
import jax.numpy as jnp
from jax import lax
from jax.experimental import pallas as pl
from jax.experimental.pallas import tpu as pltpu
from jax.sharding import PartitionSpec as P

DH = 128
HEADS = 4
NX = 4
BLK = 256
HALF = DH // 2
MESH = pl.DeviceIdType.MESH


def inner_first(left, right):
    return lax.dot_general(
        left, right, (((0,), (0,)), ((), ())), preferred_element_type=jnp.float32
    )


def inner_last(left, right):
    return lax.dot_general(
        left, right, (((1,), (1,)), ((), ())), preferred_element_type=jnp.float32
    )


def plain(left, right):
    return jnp.dot(left, right, preferred_element_type=jnp.float32)


def split(state):
    upper = state.astype(jnp.bfloat16)
    lower = (state - upper.astype(jnp.float32)).astype(jnp.bfloat16)
    return upper, lower


def kernel(
    nz, factor,
    q_hbm, k_hbm, v_hbm, g_hbm,
    att_hbm, gq_hbm, gk_hbm, gv_hbm,
    q, k, v, g,
    acc, stage,
    state, row_in, row_out, total, col_in, col_out, column, entering,
    in_sem, out_sem,
    send1, recv1, send2, recv2, send3, recv3, send4, recv4,
):
    length = q.shape[0]
    blocks = length // BLK
    me = lax.axis_index("ctx")
    z = lax.div(me, NX)
    x = lax.rem(me, NX)
    sub = HALF // nz

    def along_x(i):
        return lax.rem(x + i, NX)

    def along_z(i):
        return lax.rem(z + i, nz)

    def at(zz, xx):
        return {"ctx": zz * NX + xx}

    loads = []
    for n, (src, dst) in enumerate(((k_hbm, k), (v_hbm, v), (q_hbm, q), (g_hbm, g))):
        copy = pltpu.make_async_copy(src, dst, in_sem.at[n])
        copy.start()
        loads.append(copy)

    barrier = pltpu.get_barrier_semaphore()
    for i in range(1, NX):
        pl.semaphore_signal(barrier, inc=1, device_id=at(z, along_x(i)), device_id_type=MESH)
    for i in range(1, nz):
        pl.semaphore_signal(barrier, inc=1, device_id=at(along_z(i), x), device_id_type=MESH)

    sends = []

    def rows(half):
        return pl.ds(half * HALF, HALF)

    def send(src, dst, ssem, rsem, device):
        copy = pltpu.make_async_remote_copy(
            src_ref=src, dst_ref=dst, send_sem=ssem, recv_sem=rsem,
            device_id=device, device_id_type=MESH,
        )
        copy.start()
        sends.append(copy)

    def arrived(ref, ssem, rsem):
        pltpu.make_async_remote_copy(
            src_ref=ref, dst_ref=ref, send_sem=ssem, recv_sem=rsem,
            device_id=at(z, along_x(1)), device_id_type=MESH,
        ).wait_recv()

    def cols(h):
        if isinstance(h, int):
            return pl.ds(h * DH, DH)
        return pl.ds(pl.multiple_of(h * DH, DH), DH)

    def states(st, left, right):
        for i in (1, 3, 2):
            h = along_x(i)
            state[st, i] = inner_first(left[:, cols(h)], right[:, cols(h)])
            if st == 0 and i == 1:
                pl.semaphore_wait(barrier, NX - 1 + nz - 1)
            for half in range(2):
                send(
                    state.at[st, i, rows(half)], row_in.at[st, x, rows(half)],
                    send1.at[st, half, i], recv1.at[st, half, x], at(z, h),
                )
        row_in[st, x] = inner_first(left[:, cols(x)], right[:, cols(x)])

    def row_scan(st, half):
        for i in (1, 3, 2):
            src = along_x(i)
            arrived(row_in.at[st, src, rows(half)], send1.at[st, half, i], recv1.at[st, half, src])
        order = list(range(NX)) if st == 0 else list(reversed(range(NX)))
        run = None
        for at_x in order:
            row_out[st, at_x, rows(half)] = (
                jnp.zeros((HALF, DH), jnp.float32) if run is None else run
            )
            new = row_in[st, at_x, rows(half)]
            run = new if run is None else run + new
        run = run.reshape(nz, sub, DH)
        total[st, half] = run
        for i in range(1, nz):
            dst = along_z(i)
            send(
                total.at[st, half, dst], col_in.at[st, half, z],
                send2.at[st, half, i], recv2.at[st, half, z], at(dst, x),
            )
        col_in[st, half, z] = total[st, half, z]

    def col_scan(st, half):
        for i in range(1, nz):
            src = along_z(i)
            arrived(col_in.at[st, half, src], send2.at[st, half, i], recv2.at[st, half, src])
        order = list(range(nz)) if st == 0 else list(reversed(range(nz)))
        run = jnp.zeros((sub, DH), jnp.float32)
        for at_z in order:
            col_out[st, half, at_z] = run
            run = run + col_in[st, half, at_z]
        for i in range(1, nz):
            dst = along_z(i)
            send(
                col_out.at[st, half, dst], column.at[st, half, z],
                send3.at[st, half, i], recv3.at[st, half, z], at(dst, x),
            )
        column[st, half, z] = col_out[st, half, z]

    def give_back(st, half):
        for i in range(1, nz):
            src = along_z(i)
            arrived(column.at[st, half, src], send3.at[st, half, i], recv3.at[st, half, src])
        base = column[st, half].reshape(HALF, DH)
        for at_x in range(NX):
            row_out[st, at_x, rows(half)] += base
        for i in (1, 3, 2):
            dst = along_x(i)
            send(
                row_out.at[st, dst, rows(half)], entering.at[st, x, rows(half)],
                send4.at[st, half, i], recv4.at[st, half, x], at(z, dst),
            )
        entering[st, x, rows(half)] = row_out[st, x, rows(half)]

    def take(st, half):
        for i in (1, 3, 2):
            src = along_x(i)
            arrived(
                entering.at[st, src, rows(half)], send4.at[st, half, i], recv4.at[st, half, src]
            )

    causal = lax.broadcasted_iota(jnp.int32, (BLK, BLK), 0) >= lax.broadcasted_iota(
        jnp.int32, (BLK, BLK), 1
    )

    def unit(h, r):
        c = cols(h)
        own = pl.ds(r * BLK, BLK)
        q_r, g_r = q[own, c], g[own, c]
        until = (r + 1) * BLK

        def lower(left, right):
            parts = []
            for b in range(r + 1):
                w = inner_last(left, right[pl.ds(b * BLK, BLK), c])
                if b == r:
                    w = jnp.where(causal, w, 0.0)
                parts.append(w.astype(jnp.bfloat16))
            return parts[0] if r == 0 else jnp.concatenate(parts, axis=1)

        weights = lower(q_r, k)
        back = lower(g_r, v)
        acc[0, own, c] = plain(weights, v[:until, c])
        acc[1, own, c] = plain(back, k[:until, c])
        for n, left, right in ((2, back, q_r), (3, weights, g_r)):
            add = inner_first(left, right)
            if r > 0:
                done = r * BLK
                acc[n, :done, c] += add[:done]
                acc[n, own, c] = add[done:]
            else:
                acc[n, own, c] = add

    outs = (att_hbm, gq_hbm, gk_hbm, gv_hbm)
    stores = []

    def finish(st, h):
        c = cols(h)
        hi, lo = split(entering[st, h])
        tall = jnp.concatenate([hi, lo], axis=0)
        wide = jnp.concatenate([hi, lo], axis=1)
        pairs = ((0, q, False), (1, g, True)) if st == 0 else ((3, k, False), (2, v, True))
        for n, left, across in pairs:
            for r in range(blocks):
                own = pl.ds(r * BLK, BLK)
                lhs = left[own, c]
                lhs = jnp.concatenate([lhs, lhs], axis=1)
                inter = inner_last(lhs, wide) if across else plain(lhs, tall)
                stage[n, own, c] = (factor * (acc[n, own, c] + inter)).astype(jnp.bfloat16)
            copy = pltpu.make_async_copy(
                stage.at[n, :, c], outs[n].at[:, c], out_sem.at[n, h]
            )
            copy.start()
            stores.append(copy)

    loads[0].wait()
    loads[1].wait()
    states(0, k, v)
    loads[2].wait()
    loads[3].wait()
    states(1, q, g)

    units = [(h, r) for h in range(HEADS) for r in range(blocks)]
    steps = [
        2, (row_scan, 0, 0), 1, (row_scan, 0, 1), 1, (row_scan, 1, 0), 1, (col_scan, 0, 0),
        (row_scan, 1, 1), 1, (col_scan, 0, 1), 1, (col_scan, 1, 0), 1, (give_back, 0, 0),
        (col_scan, 1, 1), 2, (give_back, 0, 1), 2, (give_back, 1, 0), 1, (give_back, 1, 1), 16,
        (take, 0, 0), (take, 0, 1),
    ]
    for step in steps:
        if isinstance(step, int):
            for _ in range(step):
                if units:
                    unit(*units.pop(0))
        else:
            step[0](*step[1:])
    for h in range(HEADS):
        finish(0, h)
    take(1, 0)
    take(1, 1)
    for h in range(HEADS):
        finish(1, h)
    for copy in sends:
        copy.wait_send()
    for copy in stores:
        copy.wait()


def solution(mesh):
    ctx = mesh.shape["ctx"]
    nz = ctx // NX
    sub = HALF // nz

    def on_device(queries, key_vectors, value_rows, cotangent):
        length, width = queries.shape
        factor = 1.0 / math.sqrt(DH * length * ctx)
        f32 = jnp.float32
        dma = pltpu.SemaphoreType.DMA
        out = jax.ShapeDtypeStruct((length, width), jnp.bfloat16)
        return pl.pallas_call(
            functools.partial(kernel, nz, factor),
            out_shape=(out,) * 4,
            in_specs=[pl.BlockSpec(memory_space=pltpu.HBM)] * 4,
            out_specs=(pl.BlockSpec(memory_space=OUT_SPACE),) * 4,
            scratch_shapes=[pltpu.VMEM((length, width), jnp.bfloat16)] * 4
            + [
                pltpu.VMEM((4, length, width), f32),
                pltpu.VMEM((4, length, width), jnp.bfloat16),
                pltpu.VMEM((2, NX, DH, DH), f32),
                pltpu.VMEM((2, NX, DH, DH), f32),
                pltpu.VMEM((2, NX, DH, DH), f32),
                pltpu.VMEM((2, 2, nz, sub, DH), f32),
                pltpu.VMEM((2, 2, nz, sub, DH), f32),
                pltpu.VMEM((2, 2, nz, sub, DH), f32),
                pltpu.VMEM((2, 2, nz, sub, DH), f32),
                pltpu.VMEM((2, NX, DH, DH), f32),
                dma((4,)),
                dma((4, HEADS)),
                dma((2, 2, NX)), dma((2, 2, NX)),
                dma((2, 2, nz)), dma((2, 2, nz)),
                dma((2, 2, nz)), dma((2, 2, nz)),
                dma((2, 2, NX)), dma((2, 2, NX)),
            ],
            compiler_params=pltpu.CompilerParams(
                collective_id=0, has_side_effects=True, vmem_limit_bytes=40 * 1024 * 1024
            ),
            name="linear_attention",
        )(queries, key_vectors, value_rows, cotangent)

    spec = P(("grp", "ctx"), None)
    return jax.shard_map(
        on_device, mesh=mesh, in_specs=(spec,) * 4, out_specs=(spec,) * 4, check_vma=False
    )


OUT_SPACE = pltpu.HBM
```

time: 278 us -> 49.4 us (0.18)
  the two profiles are of different devices: /device:TPU:1 before, /device:TPU:8 now
where the time goes in v1:
time: 49.4 us; the launch traced here: 49.1 us
  Pallas kernels  39.7 us (80%)
  local copies, waits for them, and re-layouts  8.77 us (18%)
  between operations  0.65 us (1%)
    pallas_call x1, Pallas kernels, on_device(): pl.pallas_call(functools.partial(kernel, nz, factor), out_shape=(out,) *...  39.7 us
    unnamed x12, local copies, waits for them, and re-layouts  8.77 us

profile of v1, /device:TPU:8, one launch (start us, length us, event | category | flops | bytes accessed | tf_op | source)
XLA Modules:
  0.0 49.1 jit_solution(1915815472934984232)
XLA Ops:
  0.6 0.0 copy-start
  0.6 1.2 %copy-done = bf16[1024,512]{1,0:T(8,128)(2,1)S(1)} copy-done((bf16[1024,512]{1,0:T(8,128)(2,1)S(1)}, bf16[1024,512]{1,0:T(8,128)(2,1)}, u32[]{:S(2)}) %copy-start) | copy-done | bytes 1048600
  1.9 0.0 copy-start.1
  1.9 1.2 %copy-done.1 = bf16[1024,512]{1,0:T(8,128)(2,1)S(1)} copy-done((bf16[1024,512]{1,0:T(8,128)(2,1)S(1)}, bf16[1024,512]{1,0:T(8,128)(2,1)}, u32[]{:S(2)}) %copy-start.1) | copy-done | bytes 1048600
  3.1 0.0 copy-start.2
  3.1 1.2 %copy-done.2 = bf16[1024,512]{1,0:T(8,128)(2,1)S(1)} copy-done((bf16[1024,512]{1,0:T(8,128)(2,1)S(1)}, bf16[1024,512]{1,0:T(8,128)(2,1)}, u32[]{:S(2)}) %copy-start.2) | copy-done | bytes 1048600
  4.3 0.0 copy-start.3
  4.3 1.2 %copy-done.3 = bf16[1024,512]{1,0:T(8,128)(2,1)S(1)} copy-done((bf16[1024,512]{1,0:T(8,128)(2,1)S(1)}, bf16[1024,512]{1,0:T(8,128)(2,1)}, u32[]{:S(2)}) %copy-start.3) | copy-done | bytes 1048600
  5.5 39.7 %linear_attention.1 = (bf16[1024,512]{1,0:T(8,128)(2,1)S(1)}, bf16[1024,512]{1,0:T(8,128)(2,1)S(1)}, bf16[1024,512]{1,0:T(8,128)(2,1)S(1)}, bf16[1024,512]{1,0:T(8,128)(2,1)S(1)}) custom-call(bf16[1024,512]{1,0:T(8,128)(2,1)S(1)} %copy-done, bf16[1024,512]{1,0:T(8,128)(2,1)S(1)} %copy-done.1, bf16[1024,512]{1,0:T(8,128)(2,1)S(1)} %copy-done.2, ...), custom_call_target="tpu_custom_call" | custom-call | tf_op jit(solution)/shard_map/linear_attention/pallas_call | solution.py:275
  45.3 1.0 %copy.12 = bf16[1024,512]{1,0:T(8,128)(2,1)} copy(bf16[1024,512]{1,0:T(8,128)(2,1)S(1)} %get-tuple-element.8) | data formatting | bytes 2097152
  46.2 1.0 %copy.13 = bf16[1024,512]{1,0:T(8,128)(2,1)} copy(bf16[1024,512]{1,0:T(8,128)(2,1)S(1)} %get-tuple-element.9) | data formatting | bytes 2097152
  47.2 1.0 %copy.14 = bf16[1024,512]{1,0:T(8,128)(2,1)} copy(bf16[1024,512]{1,0:T(8,128)(2,1)S(1)} %get-tuple-element.10) | data formatting | bytes 2097152
  48.2 1.0 %copy.15 = bf16[1024,512]{1,0:T(8,128)(2,1)} copy(bf16[1024,512]{1,0:T(8,128)(2,1)S(1)} %get-tuple-element.11) | data formatting | bytes 2097152
Async XLA Ops:
  0.6 1.2 %copy-start = (bf16[1024,512]{1,0:T(8,128)(2,1)S(1)}, bf16[1024,512]{1,0:T(8,128)(2,1)}, u32[]{:S(2)}) copy-start(bf16[1024,512]{1,0:T(8,128)(2,1)} %q_hbm.1) | copy-start | bytes 3145732
  1.9 1.2 %copy-start.1 = (bf16[1024,512]{1,0:T(8,128)(2,1)S(1)}, bf16[1024,512]{1,0:T(8,128)(2,1)}, u32[]{:S(2)}) copy-start(bf16[1024,512]{1,0:T(8,128)(2,1)} %k_hbm.1) | copy-start | bytes 3145732
  3.1 1.2 %copy-start.2 = (bf16[1024,512]{1,0:T(8,128)(2,1)S(1)}, bf16[1024,512]{1,0:T(8,128)(2,1)}, u32[]{:S(2)}) copy-start(bf16[1024,512]{1,0:T(8,128)(2,1)} %v_hbm.1) | copy-start | bytes 3145732
  4.3 1.2 %copy-start.3 = (bf16[1024,512]{1,0:T(8,128)(2,1)S(1)}, bf16[1024,512]{1,0:T(8,128)(2,1)}, u32[]{:S(2)}) copy-start(bf16[1024,512]{1,0:T(8,128)(2,1)} %g_hbm.1) | copy-start | bytes 3145732

commit v2 on v1

v2 whole, which is shorter than its diff:
```python
import functools
import math

import jax
import jax.numpy as jnp
from jax import lax
from jax.experimental import pallas as pl
from jax.experimental.pallas import tpu as pltpu
from jax.sharding import PartitionSpec as P

DH = 128
HEADS = 4
NX = 4
BLK = 256
HALF = DH // 2
MESH = pl.DeviceIdType.MESH


def inner_first(left, right):
    return lax.dot_general(
        left, right, (((0,), (0,)), ((), ())), preferred_element_type=jnp.float32
    )


def inner_last(left, right):
    return lax.dot_general(
        left, right, (((1,), (1,)), ((), ())), preferred_element_type=jnp.float32
    )


def plain(left, right):
    return jnp.dot(left, right, preferred_element_type=jnp.float32)


def split(state):
    upper = state.astype(jnp.bfloat16)
    lower = (state - upper.astype(jnp.float32)).astype(jnp.bfloat16)
    return upper, lower


def kernel(
    nz, factor,
    q_hbm, k_hbm, v_hbm, g_hbm,
    att, gq, acc_k, acc_v, k, v, suffix,
    q, g, acc_a, acc_q,
    state, row_in, row_out, total, col_in, col_out, column, entering,
    in_sem,
    send1, recv1, send2, recv2, send3, recv3, send4, recv4,
):
    length = q.shape[0]
    blocks = length // BLK
    me = lax.axis_index("ctx")
    z = lax.div(me, NX)
    x = lax.rem(me, NX)
    grp = lax.axis_index("grp")
    core = lax.rem(grp, 2)
    scans = core == 1
    sub = HALF // nz

    def along_x(i):
        return lax.rem(x + i, NX)

    def along_z(i):
        return lax.rem(z + i, nz)

    def at(zz, xx, cc):
        return {"ctx": zz * NX + xx, "grp": grp - core + cc}

    def rows(half):
        return pl.ds(half * HALF, HALF)

    def cols(h):
        if isinstance(h, int):
            return pl.ds(h * DH, DH)
        return pl.ds(pl.multiple_of(h * DH, DH), DH)

    ORDER = (1, 3, 2, 0)
    loads = {}
    for n, (src, dst) in enumerate(((k_hbm, k), (v_hbm, v), (q_hbm, q), (g_hbm, g))):
        loads[n] = {}
    for pair in ((0, 1), (2, 3)):
        for i in ORDER:
            c = cols(along_x(i))
            for n in pair:
                src, dst = ((k_hbm, k), (v_hbm, v), (q_hbm, q), (g_hbm, g))[n]
                copy = pltpu.make_async_copy(src.at[:, c], dst.at[:, c], in_sem.at[n, i])
                copy.start()
                loads[n][i] = copy

    barrier = pltpu.get_barrier_semaphore()

    def greet(device):
        pl.semaphore_signal(barrier, inc=1, device_id=device, device_id_type=MESH)

    @pl.when(scans)
    def _():
        for i in range(1, NX):
            greet(at(z, along_x(i), 1))
        for i in range(NX):
            greet(at(z, along_x(i), 0))
        for i in range(1, nz):
            greet(at(along_z(i), x, 1))

    @pl.when(jnp.logical_not(scans))
    def _():
        for i in range(NX):
            greet(at(z, along_x(i), 1))

    def remote(src, dst, ssem, rsem, device):
        return pltpu.make_async_remote_copy(
            src_ref=src, dst_ref=dst, send_sem=ssem, recv_sem=rsem,
            device_id=device, device_id_type=MESH,
        )

    def arrived(ref, ssem, rsem):
        remote(ref, ref, ssem, rsem, at(z, along_x(1), 1)).wait_recv()

    def hand_in(st, half, i):
        return remote(
            state.at[st, i, rows(half)], row_in.at[core, st, x, rows(half)],
            send1.at[st, half, i], recv1.at[core, st, half, x], at(z, along_x(i), 1),
        )

    def states(st, left, right, arrays):
        for i in ORDER:
            h = along_x(i)
            for n in arrays:
                loads[n][i].wait()
            made = inner_first(left[:, cols(h)], right[:, cols(h)])
            state[st, i] = made
            if st == 0:
                if i == 1:
                    @pl.when(scans)
                    def _():
                        pl.semaphore_wait(barrier, 2 * NX - 1 + nz - 1)

                    @pl.when(jnp.logical_not(scans))
                    def _():
                        pl.semaphore_wait(barrier, NX)
                if i > 0:
                    for half in range(2):
                        hand_in(st, half, i).start()
                else:
                    hand_in_own(st, range(2))
        if st == 1:
            for half in range(2):
                for i in ORDER[:3]:
                    hand_in(st, half, i).start()
                hand_in_own(st, (half,))

    def hand_in_own(st, halves):
        @pl.when(scans)
        def _():
            for half in halves:
                row_in[1, st, x, rows(half)] = state[st, 0, rows(half)]

        @pl.when(jnp.logical_not(scans))
        def _():
            for half in halves:
                hand_in(st, half, 0).start()

    def hand_on(st, half, i):
        return remote(
            total.at[st, half, along_z(i)], col_in.at[st, half, z],
            send2.at[st, half, i], recv2.at[st, half, z], at(along_z(i), x, 1),
        )

    def row_scan(st, half):
        for cc in range(2):
            for i in ORDER[:3] if cc == 1 else ORDER:
                src = along_x(i)
                arrived(
                    row_in.at[cc, st, src, rows(half)],
                    send1.at[st, half, i], recv1.at[cc, st, half, src],
                )
        order = list(range(NX)) if st == 0 else list(reversed(range(NX)))
        for cc in range(2):
            run = None
            for at_x in order:
                row_out[cc, st, at_x, rows(half)] = (
                    jnp.zeros((HALF, DH), jnp.float32) if run is None else run
                )
                new = row_in[cc, st, at_x, rows(half)]
                run = new if run is None else run + new
            total[st, half, :, cc] = run.reshape(nz, sub, DH)
        for i in range(1, nz):
            hand_on(st, half, i).start()
        col_in[st, half, z] = total[st, half, z]

    def hand_down(st, half, i):
        return remote(
            col_out.at[st, half, along_z(i)], column.at[st, half, z],
            send3.at[st, half, i], recv3.at[st, half, z], at(along_z(i), x, 1),
        )

    def col_scan(st, half):
        for i in range(1, nz):
            src = along_z(i)
            arrived(col_in.at[st, half, src], send2.at[st, half, i], recv2.at[st, half, src])
        order = list(range(nz)) if st == 0 else list(reversed(range(nz)))
        run = jnp.zeros((2, sub, DH), jnp.float32)
        for at_z in order:
            col_out[st, half, at_z] = run
            run = run + col_in[st, half, at_z]
        for i in range(1, nz):
            hand_down(st, half, i).start()
        column[st, half, z] = col_out[st, half, z]

    def hand_back(st, half, cc, i):
        dst = along_x(i)
        return remote(
            row_out.at[cc, st, dst, rows(half)], entering.at[st, x, rows(half)],
            send4.at[cc, st, half, i], recv4.at[st, half, x], at(z, dst, cc),
        )

    def give_back(st, half):
        for i in range(1, nz):
            src = along_z(i)
            arrived(column.at[st, half, src], send3.at[st, half, i], recv3.at[st, half, src])
        for cc in range(2):
            base = column[st, half, :, cc].reshape(HALF, DH)
            for at_x in range(NX):
                row_out[cc, st, at_x, rows(half)] += base
            for i in ORDER if cc == 0 else ORDER[:3]:
                hand_back(st, half, cc, i).start()
        entering[st, x, rows(half)] = row_out[1, st, x, rows(half)]

    def take(st, half):
        for i in ORDER[:3]:
            src = along_x(i)
            arrived(
                entering.at[st, src, rows(half)], send4.at[0, st, half, i], recv4.at[st, half, src]
            )

        @pl.when(jnp.logical_not(scans))
        def _():
            arrived(entering.at[st, x, rows(half)], send4.at[0, st, half, 0], recv4.at[st, half, x])

    causal = lax.broadcasted_iota(jnp.int32, (BLK, BLK), 0) >= lax.broadcasted_iota(
        jnp.int32, (BLK, BLK), 1
    )

    def unit(h, r):
        c = cols(h)
        own = pl.ds(r * BLK, BLK)
        q_r, g_r = q[own, c], g[own, c]
        until = (r + 1) * BLK

        def lower(left, right):
            parts = []
            for b in range(r + 1):
                w = inner_last(left, right[pl.ds(b * BLK, BLK), c])
                if b == r:
                    w = jnp.where(causal, w, 0.0)
                parts.append(w.astype(jnp.bfloat16))
            return parts[0] if r == 0 else jnp.concatenate(parts, axis=1)

        weights = lower(q_r, k)
        back = lower(g_r, v)
        acc_a[own, c] = plain(weights, v[:until, c])
        acc_q[own, c] = plain(back, k[:until, c])
        for acc, left, right in ((acc_k, back, q_r), (acc_v, weights, g_r)):
            add = inner_first(left, right)
            if r > 0:
                done = r * BLK
                acc[:done, c] += add[:done]
                acc[own, c] = add[done:]
            else:
                acc[own, c] = add

    def finish(h):
        c = cols(h)
        hi, lo = split(entering[0, h])
        tall = jnp.concatenate([hi, lo], axis=0)
        wide = jnp.concatenate([hi, lo], axis=1)
        for out, acc, left in ((att, acc_a, q), (gq, acc_q, g)):
            for r in range(blocks):
                own = pl.ds(r * BLK, BLK)
                lhs = left[own, c]
                lhs = jnp.concatenate([lhs, lhs], axis=1)
                inter = plain(lhs, tall) if left is q else inner_last(lhs, wide)
                out[own, c] = (factor * (acc[own, c] + inter)).astype(jnp.bfloat16)

    states(0, k, v, (0, 1))
    states(1, q, g, (2, 3))

    units = [(h, r) for h in range(HEADS) for r in range(blocks)]
    steps = [
        3, (row_scan, 0, 0), (row_scan, 0, 1), 1, (row_scan, 1, 0), 1, (row_scan, 1, 1), 1,
        (col_scan, 0, 0), (col_scan, 0, 1), 1, (col_scan, 1, 0), 2, (col_scan, 1, 1), 1,
        (give_back, 0, 0), (give_back, 0, 1), 2, (give_back, 1, 0), 2, (give_back, 1, 1), 16,
    ]
    for step in steps:
        if isinstance(step, int):
            for _ in range(step):
                if units:
                    unit(*units.pop(0))
        else:
            pl.when(scans)(functools.partial(*step))
    take(0, 0)
    take(0, 1)
    for h in range(HEADS):
        finish(h)
    take(1, 0)
    take(1, 1)
    for h in range(HEADS):
        suffix[h, 0], suffix[h, 1] = split(entering[1, h])

    for st in range(2):
        for half in range(2):
            for i in range(1, NX):
                hand_in(st, half, i).wait_send()

    @pl.when(jnp.logical_not(scans))
    def _():
        for st in range(2):
            for half in range(2):
                hand_in(st, half, 0).wait_send()

    @pl.when(scans)
    def _():
        for st in range(2):
            for half in range(2):
                for i in range(1, nz):
                    hand_on(st, half, i).wait_send()
                    hand_down(st, half, i).wait_send()
                for i in range(NX):
                    hand_back(st, half, 0, i).wait_send()
                for i in range(1, NX):
                    hand_back(st, half, 1, i).wait_send()


def last_part(
    factor,
    att, gq, acc_k, acc_v, k, v, suffix,
    att_hbm, gq_hbm, gk_hbm, gv_hbm,
    gk, gv, sem,
):
    length = k.shape[0]
    copies = []

    def write(n, src, dst, part):
        copy = pltpu.make_async_copy(src.at[part], dst.at[part], sem.at[n, part.start // BLK])
        copy.start()
        copies.append(copy)

    parts = [pl.ds(r * BLK, BLK) for r in range(length // BLK)]
    for own in parts:
        write(0, att, att_hbm, own)
        write(1, gq, gq_hbm, own)
    for own in parts:
        for h in range(HEADS):
            c = pl.ds(h * DH, DH)
            tall = jnp.concatenate([suffix[h, 0], suffix[h, 1]], axis=0)
            wide = jnp.concatenate([suffix[h, 0], suffix[h, 1]], axis=1)
            lhs = k[own, c]
            inter = plain(jnp.concatenate([lhs, lhs], axis=1), tall)
            gv[own, c] = (factor * (acc_v[own, c] + inter)).astype(jnp.bfloat16)
            lhs = v[own, c]
            inter = inner_last(jnp.concatenate([lhs, lhs], axis=1), wide)
            gk[own, c] = (factor * (acc_k[own, c] + inter)).astype(jnp.bfloat16)
        write(2, gk, gk_hbm, own)
        write(3, gv, gv_hbm, own)
    for copy in copies:
        copy.wait()


def solution(mesh):
    ctx = mesh.shape["ctx"]
    nz = ctx // NX
    sub = HALF // nz

    def on_device(queries, key_vectors, value_rows, cotangent):
        length, width = queries.shape
        factor = 1.0 / math.sqrt(DH * length * ctx)
        f32, bf16 = jnp.float32, jnp.bfloat16
        dma = pltpu.SemaphoreType.DMA
        vmem, hbm = pltpu.VMEM, pltpu.HBM
        ready = pl.pallas_call(
            functools.partial(kernel, nz, factor),
            out_shape=(
                vmem((length, width), bf16),
                vmem((length, width), bf16),
                vmem((length, width), f32),
                vmem((length, width), f32),
                vmem((length, width), bf16),
                vmem((length, width), bf16),
                vmem((HEADS, 2, DH, DH), bf16),
            ),
            in_specs=[pl.BlockSpec(memory_space=hbm)] * 4,
            out_specs=(pl.BlockSpec(memory_space=vmem),) * 7,
            scratch_shapes=[
                vmem((length, width), bf16),
                vmem((length, width), bf16),
                vmem((length, width), f32),
                vmem((length, width), f32),
                vmem((2, NX, DH, DH), f32),
                vmem((2, 2, NX, DH, DH), f32),
                vmem((2, 2, NX, DH, DH), f32),
                vmem((2, 2, nz, 2, sub, DH), f32),
                vmem((2, 2, nz, 2, sub, DH), f32),
                vmem((2, 2, nz, 2, sub, DH), f32),
                vmem((2, 2, nz, 2, sub, DH), f32),
                vmem((2, NX, DH, DH), f32),
                dma((4, NX)),
                dma((2, 2, NX)), dma((2, 2, 2, NX)),
                dma((2, 2, nz)), dma((2, 2, nz)),
                dma((2, 2, nz)), dma((2, 2, nz)),
                dma((2, 2, 2, NX)), dma((2, 2, NX)),
            ],
            compiler_params=pltpu.CompilerParams(
                collective_id=0, has_side_effects=True, vmem_limit_bytes=32 * 1024 * 1024
            ),
            name="linear_attention",
        )(*(
            pltpu.with_memory_space_constraint(arr, hbm)
            for arr in (queries, key_vectors, value_rows, cotangent)
        ))
        out = jax.ShapeDtypeStruct((length, width), bf16)
        return pl.pallas_call(
            functools.partial(last_part, factor),
            out_shape=(out,) * 4,
            in_specs=[pl.BlockSpec(memory_space=vmem)] * 7,
            out_specs=(pl.BlockSpec(memory_space=hbm),) * 4,
            scratch_shapes=[
                vmem((length, width), bf16),
                vmem((length, width), bf16),
                dma((4, length // BLK)),
            ],
            compiler_params=pltpu.CompilerParams(vmem_limit_bytes=16 * 1024 * 1024),
            name="last_part",
        )(*(pltpu.with_memory_space_constraint(arr, vmem) for arr in ready))

    spec = P(("grp", "ctx"), None)
    return jax.shard_map(
        on_device, mesh=mesh, in_specs=(spec,) * 4, out_specs=(spec,) * 4, check_vma=False
    )
```

time: 49.4 us -> 35.2 us (0.71)
  the two profiles are of different devices: /device:TPU:8 before, /device:TPU:1 now
where the time goes in v2:
time: 35.2 us; the launch traced here: 35.1 us
  Pallas kernels  34.3 us (97%)
  between operations  0.8 us (2%)
    pallas_call x1, Pallas kernels, on_device(): pl.pallas_call(functools.partial(kernel, nz, factor), out_shape=(vmem((le...  32.1 us
    pallas_call x1, Pallas kernels, on_device(): pl.pallas_call(functools.partial(last_part, factor), out_shape=(out,) * 4...  2.18 us

profile of v2, /device:TPU:1, one launch (start us, length us, event | category | flops | bytes accessed | tf_op | source)
XLA Modules:
  0.0 35.1 jit_solution(7682880313456841207)
XLA Ops:
  0.6 32.1 %linear_attention.1 = (bf16[1024,512]{1,0:T(8,128)(2,1)S(1)}, bf16[1024,512]{1,0:T(8,128)(2,1)S(1)}, f32[1024,512]{1,0:T(8,128)S(1)}, f32[1024,512]{1,0:T(8,128)...) custom-call(bf16[1024,512]{1,0:T(8,128)(2,1)} %q_hbm.1, ...), custom_call_target="tpu_custom_call" | custom-call | tf_op jit(solution)/shard_map/linear_attention/pallas_call | solution.py:379
  32.8 2.2 %last_part.1 = (bf16[1024,512]{1,0:T(8,128)(2,1)}, bf16[1024,512]{1,0:T(8,128)(2,1)}, bf16[1024,512]{1,0:T(8,128)(2,1)}, bf16[1024,512]{1,0:T(8,128)(2,1)}) custom-call(bf16[1024,512]{1,0:T(8,128)(2,1)S(1)} %get-tuple-element.11.att, bf16[1024,512]{1,0:T(8,128)(2,1)S(1)} %get-tuple-element.12.gq, f32[1024,512]{1,0:T(8,128)S(1)} %get-tuple-element.13.acc_k, ...), custom_call_target="tpu_custom_call" | custom-call | tf_op jit(solution)/shard_map/last_part/pallas_call | solution.py:420

commit v3 on v2

v3 whole, which is shorter than its diff:
```python
import functools
import math

import jax
import jax.numpy as jnp
from jax import lax
from jax.experimental import pallas as pl
from jax.experimental.pallas import tpu as pltpu
from jax.sharding import PartitionSpec as P

DH = 128
HEADS = 4
NX = 4
BLK = 256
PIECES = 2
TALL = DH // PIECES
MESH = pl.DeviceIdType.MESH


def inner_first(left, right):
    return lax.dot_general(
        left, right, (((0,), (0,)), ((), ())), preferred_element_type=jnp.float32
    )


def inner_last(left, right):
    return lax.dot_general(
        left, right, (((1,), (1,)), ((), ())), preferred_element_type=jnp.float32
    )


def plain(left, right):
    return jnp.dot(left, right, preferred_element_type=jnp.float32)


def split(state):
    upper = state.astype(jnp.bfloat16)
    lower = (state - upper.astype(jnp.float32)).astype(jnp.bfloat16)
    return upper, lower


def kernel(
    nz, factor,
    q_hbm, k_hbm, v_hbm, g_hbm,
    att, gq, acc_k, acc_v, k, v, suffix,
    q, g, acc_a, acc_q,
    state, row_in, row_out, total, col_in, col_out, column, entering,
    in_sem, sent, got1, got2, got3, got4,
):
    length = q.shape[0]
    blocks = length // BLK
    me = lax.axis_index("ctx")
    z = lax.div(me, NX)
    x = lax.rem(me, NX)
    grp = lax.axis_index("grp")
    core = lax.rem(grp, 2)
    scans = core == 1
    sub = TALL // nz

    def along_x(i):
        return lax.rem(x + i, NX)

    def along_z(i):
        return lax.rem(z + i, nz)

    def at(zz, xx, cc):
        return {"ctx": zz * NX + xx, "grp": grp - core + cc}

    def rows(part):
        return pl.ds(part * TALL, TALL)

    def cols(h):
        if isinstance(h, int):
            return pl.ds(h * DH, DH)
        return pl.ds(pl.multiple_of(h * DH, DH), DH)

    loads = []
    for n, (src, dst) in enumerate(((k_hbm, k), (v_hbm, v), (q_hbm, q), (g_hbm, g))):
        copy = pltpu.make_async_copy(src, dst, in_sem.at[n])
        copy.start()
        loads.append(copy)

    barrier = pltpu.get_barrier_semaphore()

    def greet(device):
        pl.semaphore_signal(barrier, inc=1, device_id=device, device_id_type=MESH)

    @pl.when(scans)
    def _():
        for i in range(1, NX):
            greet(at(z, along_x(i), 1))
        for i in range(NX):
            greet(at(z, along_x(i), 0))
        for i in range(1, nz):
            greet(at(along_z(i), x, 1))

    @pl.when(jnp.logical_not(scans))
    def _():
        for i in range(NX):
            greet(at(z, along_x(i), 1))

    def send(src, dst, ssem, rsem, device):
        pltpu.make_async_remote_copy(
            src_ref=src, dst_ref=dst, send_sem=ssem, recv_sem=rsem,
            device_id=device, device_id_type=MESH,
        ).start()

    def arrived(ref, sem):
        pltpu.make_async_copy(ref, ref, sem).wait()

    ORDER = (1, 3, 2, 0)

    def hand_in(st, part, i):
        send(
            state.at[st, i, rows(part)], row_in.at[st, part, core * NX + x],
            sent.at[0], got1.at[st, part], at(z, along_x(i), 1),
        )

    def hand_in_own(st, part):
        @pl.when(scans)
        def _():
            row_in[st, part, NX + x] = state[st, 0, rows(part)]

        @pl.when(jnp.logical_not(scans))
        def _():
            hand_in(st, part, 0)

    def states(st, left, right):
        for i in ORDER:
            h = along_x(i)
            state[st, i] = inner_first(left[:, cols(h)], right[:, cols(h)])
            if st == 0:
                if i == 1:
                    @pl.when(scans)
                    def _():
                        pl.semaphore_wait(barrier, 2 * NX - 1 + nz - 1)

                    @pl.when(jnp.logical_not(scans))
                    def _():
                        pl.semaphore_wait(barrier, NX)
                for part in range(PIECES):
                    hand_in(st, part, i) if i > 0 else hand_in_own(st, part)
        if st == 1:
            for part in range(PIECES):
                for i in ORDER[:3]:
                    hand_in(st, part, i)
                hand_in_own(st, part)

    def row_scan(st, part):
        arrived(row_in.at[st, part, pl.ds(0, 2 * NX - 1)], got1.at[st, part])
        order = list(range(NX)) if st == 0 else list(reversed(range(NX)))
        for cc in range(2):
            run = None
            for at_x in order:
                row_out[cc, st, at_x, rows(part)] = (
                    jnp.zeros((TALL, DH), jnp.float32) if run is None else run
                )
                new = row_in[st, part, cc * NX + at_x]
                run = new if run is None else run + new
            total[st, part, :, cc] = run.reshape(nz, sub, DH)
        for i in range(1, nz):
            send(
                total.at[st, part, along_z(i)], col_in.at[st, part, z],
                sent.at[1], got2.at[st, part], at(along_z(i), x, 1),
            )
        col_in[st, part, z] = total[st, part, z]

    def col_scan(st, part):
        arrived(col_in.at[st, part, pl.ds(0, nz - 1)], got2.at[st, part])
        order = list(range(nz)) if st == 0 else list(reversed(range(nz)))
        run = jnp.zeros((2, sub, DH), jnp.float32)
        for at_z in order:
            col_out[st, part, at_z] = run
            run = run + col_in[st, part, at_z]
        for i in range(1, nz):
            send(
                col_out.at[st, part, along_z(i)], column.at[st, part, z],
                sent.at[2], got3.at[st, part], at(along_z(i), x, 1),
            )
        column[st, part, z] = col_out[st, part, z]

    def give_back(st, part):
        arrived(column.at[st, part, pl.ds(0, nz - 1)], got3.at[st, part])
        for cc in range(2):
            base = column[st, part, :, cc].reshape(TALL, DH)
            for at_x in range(NX):
                row_out[cc, st, at_x, rows(part)] += base
            for i in ORDER if cc == 0 else ORDER[:3]:
                send(
                    row_out.at[cc, st, along_x(i), rows(part)], entering.at[st, part, x],
                    sent.at[3 + cc], got4.at[st, part], at(z, along_x(i), cc),
                )
        entering[st, part, x] = row_out[1, st, x, rows(part)]

    def take(st, part):
        @pl.when(scans)
        def _():
            arrived(entering.at[st, part, pl.ds(0, NX - 1)], got4.at[st, part])

        @pl.when(jnp.logical_not(scans))
        def _():
            arrived(entering.at[st, part], got4.at[st, part])

    def entered(st, h):
        return jnp.concatenate([entering[st, part, h] for part in range(PIECES)], axis=0)

    causal = lax.broadcasted_iota(jnp.int32, (BLK, BLK), 0) >= lax.broadcasted_iota(
        jnp.int32, (BLK, BLK), 1
    )

    def unit(h, r):
        c = cols(h)
        own = pl.ds(r * BLK, BLK)
        q_r, g_r = q[own, c], g[own, c]
        until = (r + 1) * BLK

        def lower(left, right):
            parts = []
            for b in range(r + 1):
                w = inner_last(left, right[pl.ds(b * BLK, BLK), c])
                if b == r:
                    w = jnp.where(causal, w, 0.0)
                parts.append(w.astype(jnp.bfloat16))
            return parts[0] if r == 0 else jnp.concatenate(parts, axis=1)

        weights = lower(q_r, k)
        back = lower(g_r, v)
        acc_a[own, c] = plain(weights, v[:until, c])
        acc_q[own, c] = plain(back, k[:until, c])
        for acc, left, right in ((acc_k, back, q_r), (acc_v, weights, g_r)):
            add = inner_first(left, right)
            if r > 0:
                done = r * BLK
                acc[:done, c] += add[:done]
                acc[own, c] = add[done:]
            else:
                acc[own, c] = add

    def finish(h):
        c = cols(h)
        hi, lo = split(entered(0, h))
        tall = jnp.concatenate([hi, lo], axis=0)
        wide = jnp.concatenate([hi, lo], axis=1)
        for out, acc, left in ((att, acc_a, q), (gq, acc_q, g)):
            for r in range(blocks):
                own = pl.ds(r * BLK, BLK)
                lhs = left[own, c]
                lhs = jnp.concatenate([lhs, lhs], axis=1)
                inter = plain(lhs, tall) if left is q else inner_last(lhs, wide)
                out[own, c] = (factor * (acc[own, c] + inter)).astype(jnp.bfloat16)

    loads[0].wait()
    loads[1].wait()
    states(0, k, v)
    loads[2].wait()
    loads[3].wait()
    states(1, q, g)

    units = [(h, r) for h in range(HEADS) for r in range(blocks)]
    steps = [
        3, (row_scan, 0, 0), (row_scan, 0, 1), 1, (row_scan, 1, 0), 1, (row_scan, 1, 1), 1,
        (col_scan, 0, 0), (col_scan, 0, 1), 1, (col_scan, 1, 0), 2, (col_scan, 1, 1), 1,
        (give_back, 0, 0), (give_back, 0, 1), 2, (give_back, 1, 0), 2, (give_back, 1, 1), 16,
    ]
    for step in steps:
        if isinstance(step, int):
            for _ in range(step):
                if units:
                    unit(*units.pop(0))
        else:
            pl.when(scans)(functools.partial(*step))
    for part in range(PIECES):
        take(0, part)
    for h in range(HEADS):
        finish(h)
    for part in range(PIECES):
        take(1, part)
    for h in range(HEADS):
        suffix[h, 0], suffix[h, 1] = split(entered(1, h))

    def gone(ref, n):
        pltpu.make_async_copy(ref, ref, sent.at[n]).wait()

    @pl.when(scans)
    def _():
        gone(state.at[:, pl.ds(0, NX - 1)], 0)
        gone(total.at[:, :, pl.ds(0, nz - 1)], 1)
        gone(col_out.at[:, :, pl.ds(0, nz - 1)], 2)
        gone(row_out.at[0], 3)
        gone(row_out.at[1, :, pl.ds(0, NX - 1)], 4)

    @pl.when(jnp.logical_not(scans))
    def _():
        gone(state, 0)


def last_part(
    factor,
    att, gq, acc_k, acc_v, k, v, suffix,
    att_hbm, gq_hbm, gk_hbm, gv_hbm,
    gk, gv, sem,
):
    length = k.shape[0]
    copies = []

    def write(n, src, dst, part):
        copy = pltpu.make_async_copy(src.at[part], dst.at[part], sem.at[n, part.start // BLK])
        copy.start()
        copies.append(copy)

    parts = [pl.ds(r * BLK, BLK) for r in range(length // BLK)]
    for own in parts:
        write(0, att, att_hbm, own)
        write(1, gq, gq_hbm, own)
    for own in parts:
        for h in range(HEADS):
            c = pl.ds(h * DH, DH)
            tall = jnp.concatenate([suffix[h, 0], suffix[h, 1]], axis=0)
            wide = jnp.concatenate([suffix[h, 0], suffix[h, 1]], axis=1)
            lhs = k[own, c]
            inter = plain(jnp.concatenate([lhs, lhs], axis=1), tall)
            gv[own, c] = (factor * (acc_v[own, c] + inter)).astype(jnp.bfloat16)
            lhs = v[own, c]
            inter = inner_last(jnp.concatenate([lhs, lhs], axis=1), wide)
            gk[own, c] = (factor * (acc_k[own, c] + inter)).astype(jnp.bfloat16)
        write(2, gk, gk_hbm, own)
        write(3, gv, gv_hbm, own)
    for copy in copies:
        copy.wait()


def solution(mesh):
    ctx = mesh.shape["ctx"]
    nz = ctx // NX
    sub = TALL // nz

    def on_device(queries, key_vectors, value_rows, cotangent):
        length, width = queries.shape
        factor = 1.0 / math.sqrt(DH * length * ctx)
        f32, bf16 = jnp.float32, jnp.bfloat16
        dma = pltpu.SemaphoreType.DMA
        vmem, hbm = pltpu.VMEM, pltpu.HBM
        ready = pl.pallas_call(
            functools.partial(kernel, nz, factor),
            out_shape=(
                vmem((length, width), bf16),
                vmem((length, width), bf16),
                vmem((length, width), f32),
                vmem((length, width), f32),
                vmem((length, width), bf16),
                vmem((length, width), bf16),
                vmem((HEADS, 2, DH, DH), bf16),
            ),
            in_specs=[pl.BlockSpec(memory_space=hbm)] * 4,
            out_specs=(pl.BlockSpec(memory_space=vmem),) * 7,
            scratch_shapes=[
                vmem((length, width), bf16),
                vmem((length, width), bf16),
                vmem((length, width), f32),
                vmem((length, width), f32),
                vmem((2, NX, DH, DH), f32),
                vmem((2, PIECES, 2 * NX, TALL, DH), f32),
                vmem((2, 2, NX, DH, DH), f32),
                vmem((2, PIECES, nz, 2, sub, DH), f32),
                vmem((2, PIECES, nz, 2, sub, DH), f32),
                vmem((2, PIECES, nz, 2, sub, DH), f32),
                vmem((2, PIECES, nz, 2, sub, DH), f32),
                vmem((2, PIECES, NX, TALL, DH), f32),
                dma((4,)),
                dma((5,)),
                dma((2, PIECES)), dma((2, PIECES)), dma((2, PIECES)), dma((2, PIECES)),
            ],
            compiler_params=pltpu.CompilerParams(
                collective_id=0, has_side_effects=True, vmem_limit_bytes=32 * 1024 * 1024
            ),
            name="linear_attention",
        )(*(
            pltpu.with_memory_space_constraint(arr, hbm)
            for arr in (queries, key_vectors, value_rows, cotangent)
        ))
        out = jax.ShapeDtypeStruct((length, width), bf16)
        return pl.pallas_call(
            functools.partial(last_part, factor),
            out_shape=(out,) * 4,
            in_specs=[pl.BlockSpec(memory_space=vmem)] * 7,
            out_specs=(pl.BlockSpec(memory_space=hbm),) * 4,
            scratch_shapes=[
                vmem((length, width), bf16),
                vmem((length, width), bf16),
                dma((4, length // BLK)),
            ],
            compiler_params=pltpu.CompilerParams(vmem_limit_bytes=16 * 1024 * 1024),
            name="last_part",
        )(*(pltpu.with_memory_space_constraint(arr, vmem) for arr in ready))

    spec = P(("grp", "ctx"), None)
    return jax.shard_map(
        on_device, mesh=mesh, in_specs=(spec,) * 4, out_specs=(spec,) * 4, check_vma=False
    )
```

time: 35.2 us -> 33.1 us (0.940)
  Pallas kernels: 34.3 us -> 32.2 us
    pallas_call x1, Pallas kernels: 32.1 us -> 30.1 us  [on_device(): pl.pallas_call(functools.partial(kernel, nz, factor), out_shape=(vmem((le...]
where the time goes in v3:
time: 33.1 us; the launch traced here: 33 us
  Pallas kernels  32.2 us (97%)
  between operations  0.8 us (2%)
    pallas_call x1, Pallas kernels, on_device(): pl.pallas_call(functools.partial(kernel, nz, factor), out_shape=(vmem((le...  30.1 us
    pallas_call x1, Pallas kernels, on_device(): pl.pallas_call(functools.partial(last_part, factor), out_shape=(out,) * 4...  2.17 us

profile of v3, /device:TPU:1, one launch (start us, length us, event | category | flops | bytes accessed | tf_op | source)
XLA Modules:
  0.0 33.0 jit_solution(13304311341742922859)
XLA Ops:
  0.6 30.1 %linear_attention.1 = (bf16[1024,512]{1,0:T(8,128)(2,1)S(1)}, bf16[1024,512]{1,0:T(8,128)(2,1)S(1)}, f32[1024,512]{1,0:T(8,128)S(1)}, f32[1024,512]{1,0:T(8,128)...) custom-call(bf16[1024,512]{1,0:T(8,128)(2,1)} %q_hbm.1, ...), custom_call_target="tpu_custom_call" | custom-call | tf_op jit(solution)/shard_map/linear_attention/pallas_call | solution.py:343
  30.7 2.2 %last_part.1 = (bf16[1024,512]{1,0:T(8,128)(2,1)}, bf16[1024,512]{1,0:T(8,128)(2,1)}, bf16[1024,512]{1,0:T(8,128)(2,1)}, bf16[1024,512]{1,0:T(8,128)(2,1)}) custom-call(bf16[1024,512]{1,0:T(8,128)(2,1)S(1)} %get-tuple-element.11.att, bf16[1024,512]{1,0:T(8,128)(2,1)S(1)} %get-tuple-element.12.gq, f32[1024,512]{1,0:T(8,128)S(1)} %get-tuple-element.13.acc_k, ...), custom_call_target="tpu_custom_call" | custom-call | tf_op jit(solution)/shard_map/last_part/pallas_call | solution.py:382

commit v4 on v3

--- a/solution.py
+++ b/solution.py
@@ -13,6 +13,7 @@
 NX = 4
 BLK = 256
 PIECES = 2
+FEW = 3
 TALL = DH // PIECES
 MESH = pl.DeviceIdType.MESH
 
@@ -45,7 +46,7 @@
     att, gq, acc_k, acc_v, k, v, suffix,
     q, g, acc_a, acc_q,
     state, row_in, row_out, total, col_in, col_out, column, entering,
-    in_sem, sent, got1, got2, got3, got4,
+    in_sem, sent, got1, got2, got3, got4, ready,
 ):
     length = q.shape[0]
     blocks = length // BLK
@@ -74,30 +75,35 @@
             return pl.ds(h * DH, DH)
         return pl.ds(pl.multiple_of(h * DH, DH), DH)
 
-    loads = []
-    for n, (src, dst) in enumerate(((k_hbm, k), (v_hbm, v), (q_hbm, q), (g_hbm, g))):
-        copy = pltpu.make_async_copy(src, dst, in_sem.at[n])
-        copy.start()
-        loads.append(copy)
+    early = z < FEW
+
+    def load(n):
+        src, dst = ((k_hbm, k), (v_hbm, v), (q_hbm, q), (g_hbm, g))[n]
+        return pltpu.make_async_copy(src, dst, in_sem.at[n])
+
+    @pl.when(early)
+    def _():
+        for n in (0, 1, 2, 3):
+            load(n).start()
+
+    @pl.when(jnp.logical_not(early))
+    def _():
+        for n in (2, 3, 0, 1):
+            load(n).start()
 
     barrier = pltpu.get_barrier_semaphore()
 
-    def greet(device):
-        pl.semaphore_signal(barrier, inc=1, device_id=device, device_id_type=MESH)
-
     @pl.when(scans)
     def _():
-        for i in range(1, NX):
-            greet(at(z, along_x(i), 1))
         for i in range(NX):
-            greet(at(z, along_x(i), 0))
+            pl.semaphore_signal(barrier, inc=1, device_id=at(z, along_x(i), 0), device_id_type=MESH)
         for i in range(1, nz):
-            greet(at(along_z(i), x, 1))
+            pl.semaphore_signal(barrier, inc=1, device_id=at(along_z(i), x, 1), device_id_type=MESH)
 
     @pl.when(jnp.logical_not(scans))
     def _():
-        for i in range(NX):
-            greet(at(z, along_x(i), 1))
+        pl.semaphore_wait(barrier, NX)
+        pl.semaphore_signal(ready, inc=1, device_id=at(z, x, 1), device_id_type=MESH)
 
     def send(src, dst, ssem, rsem, device):
         pltpu.make_async_remote_copy(
@@ -125,28 +131,27 @@
         def _():
             hand_in(st, part, 0)
 
-    def states(st, left, right):
+    def states(st, first):
+        left, right = ((k, v), (q, g))[st]
+        load(2 * st).wait()
+        load(2 * st + 1).wait()
         for i in ORDER:
             h = along_x(i)
             state[st, i] = inner_first(left[:, cols(h)], right[:, cols(h)])
-            if st == 0:
+            if first:
                 if i == 1:
                     @pl.when(scans)
                     def _():
-                        pl.semaphore_wait(barrier, 2 * NX - 1 + nz - 1)
-
-                    @pl.when(jnp.logical_not(scans))
-                    def _():
-                        pl.semaphore_wait(barrier, NX)
+                        pl.semaphore_wait(ready, 1)
                 for part in range(PIECES):
                     hand_in(st, part, i) if i > 0 else hand_in_own(st, part)
-        if st == 1:
+        if not first:
             for part in range(PIECES):
                 for i in ORDER[:3]:
                     hand_in(st, part, i)
                 hand_in_own(st, part)
 
-    def row_scan(st, part):
+    def row_scan(st, part, meet=False):
         arrived(row_in.at[st, part, pl.ds(0, 2 * NX - 1)], got1.at[st, part])
         order = list(range(NX)) if st == 0 else list(reversed(range(NX)))
         for cc in range(2):
@@ -158,39 +163,98 @@
                 new = row_in[st, part, cc * NX + at_x]
                 run = new if run is None else run + new
             total[st, part, :, cc] = run.reshape(nz, sub, DH)
+        if meet:
+            pl.semaphore_wait(barrier, nz - 1)
         for i in range(1, nz):
             send(
                 total.at[st, part, along_z(i)], col_in.at[st, part, z],
-                sent.at[1], got2.at[st, part], at(along_z(i), x, 1),
+                sent.at[1], got2.at[st, part, jnp.where(early, 0, 1)], at(along_z(i), x, 1),
             )
         col_in[st, part, z] = total[st, part, z]
 
-    def col_scan(st, part):
-        arrived(col_in.at[st, part, pl.ds(0, nz - 1)], got2.at[st, part])
-        order = list(range(nz)) if st == 0 else list(reversed(range(nz)))
+    def heard(st, part, few):
+        group = got2.at[st, part, 0 if few else 1]
+        among = FEW if few else nz - FEW
+        inside = early if few else jnp.logical_not(early)
+
+        @pl.when(inside)
+        def _():
+            arrived(col_in.at[st, part, pl.ds(0, among - 1)], group)
+
+        @pl.when(jnp.logical_not(inside))
+        def _():
+            arrived(col_in.at[st, part, pl.ds(0, among)], group)
+
+    def tell(st, part, dst):
+        @pl.when(z != dst)
+        def _():
+            send(
+                col_out.at[st, part, dst], column.at[st, part, z],
+                sent.at[2], got3.at[st, part], at(dst, x, 1),
+            )
+
+    def col_scan(part):
+        heard(1, part, True)
+        heard(1, part, False)
         run = jnp.zeros((2, sub, DH), jnp.float32)
-        for at_z in order:
-            col_out[st, part, at_z] = run
-            run = run + col_in[st, part, at_z]
-        for i in range(1, nz):
-            send(
-                col_out.at[st, part, along_z(i)], column.at[st, part, z],
-                sent.at[2], got3.at[st, part], at(along_z(i), x, 1),
-            )
-        column[st, part, z] = col_out[st, part, z]
-
-    def give_back(st, part):
-        arrived(column.at[st, part, pl.ds(0, nz - 1)], got3.at[st, part])
+        for at_z in reversed(range(nz)):
+            col_out[1, part, at_z] = run
+            run = run + col_in[1, part, at_z]
+        for at_z in range(nz):
+            tell(1, part, at_z)
+        column[1, part, z] = col_out[1, part, z]
+
+    def col_scan_few(part):
+        heard(0, part, True)
+        run = jnp.zeros((2, sub, DH), jnp.float32)
+        for at_z in range(FEW):
+            run = run + col_in[0, part, at_z]
+            col_out[0, part, at_z + 1] = run
+        for at_z in range(1, FEW + 1):
+            tell(0, part, at_z)
+
+    def col_scan_rest(part):
+        heard(0, part, False)
+        run = col_out[0, part, FEW]
+        for at_z in range(FEW, nz - 1):
+            run = run + col_in[0, part, at_z]
+            col_out[0, part, at_z + 1] = run
+        for at_z in range(FEW + 1, nz):
+            tell(0, part, at_z)
+
+    def give_back(st, part, alone=False):
+        if not alone:
+            if st == 0:
+                column[0, part, z] = col_out[0, part, z]
+            arrived(column.at[st, part, pl.ds(0, nz - 1)], got3.at[st, part])
         for cc in range(2):
-            base = column[st, part, :, cc].reshape(TALL, DH)
-            for at_x in range(NX):
-                row_out[cc, st, at_x, rows(part)] += base
-            for i in ORDER if cc == 0 else ORDER[:3]:
-                send(
-                    row_out.at[cc, st, along_x(i), rows(part)], entering.at[st, part, x],
-                    sent.at[3 + cc], got4.at[st, part], at(z, along_x(i), cc),
-                )
+            if not alone:
+                base = column[st, part, :, cc].reshape(TALL, DH)
+            for i in (2, 1, 3, 0):
+                here = row_out.at[cc, st, along_x(i), rows(part)]
+                if not alone:
+                    here[...] += base
+                if cc == 0 or i > 0:
+                    send(
+                        here, entering.at[st, part, x],
+                        sent.at[3 + cc], got4.at[st, part], at(z, along_x(i), cc),
+                    )
         entering[st, part, x] = row_out[1, st, x, rows(part)]
+
+    def give_first(part):
+        @pl.when(z == 0)
+        def _():
+            give_back(0, part, True)
+
+    def give_few(part):
+        @pl.when(jnp.logical_and(z > 0, z <= FEW))
+        def _():
+            give_back(0, part)
+
+    def give_rest(part):
+        @pl.when(z > FEW)
+        def _():
+            give_back(0, part)
 
     def take(st, part):
         @pl.when(scans)
@@ -249,18 +313,49 @@
                 inter = plain(lhs, tall) if left is q else inner_last(lhs, wide)
                 out[own, c] = (factor * (acc[own, c] + inter)).astype(jnp.bfloat16)
 
-    loads[0].wait()
-    loads[1].wait()
-    states(0, k, v)
-    loads[2].wait()
-    loads[3].wait()
-    states(1, q, g)
+    @pl.when(early)
+    def _():
+        states(0, True)
+        states(1, False)
+
+    @pl.when(jnp.logical_not(early))
+    def _():
+        states(1, True)
+        states(0, False)
+
+    def first_scans():
+        @pl.when(early)
+        def _():
+            for part in range(PIECES):
+                row_scan(0, part, part == 0)
+
+        @pl.when(jnp.logical_not(early))
+        def _():
+            for part in range(PIECES):
+                row_scan(1, part, part == 0)
+
+    def second_scans():
+        @pl.when(early)
+        def _():
+            for part in range(PIECES):
+                row_scan(1, part)
+            for part in range(PIECES):
+                give_first(part)
+            for part in range(PIECES):
+                col_scan_few(part)
+
+        @pl.when(jnp.logical_not(early))
+        def _():
+            for part in range(PIECES):
+                col_scan_few(part)
+            for part in range(PIECES):
+                row_scan(0, part)
 
     units = [(h, r) for h in range(HEADS) for r in range(blocks)]
     steps = [
-        3, (row_scan, 0, 0), (row_scan, 0, 1), 1, (row_scan, 1, 0), 1, (row_scan, 1, 1), 1,
-        (col_scan, 0, 0), (col_scan, 0, 1), 1, (col_scan, 1, 0), 2, (col_scan, 1, 1), 1,
-        (give_back, 0, 0), (give_back, 0, 1), 2, (give_back, 1, 0), 2, (give_back, 1, 1), 16,
+        6, (first_scans,), 3, (second_scans,), (col_scan, 0), (col_scan, 1), 3,
+        (give_few, 0), (give_few, 1), (col_scan_rest, 0), (col_scan_rest, 1), 1,
+        (give_back, 1, 0), (give_back, 1, 1), 2, (give_rest, 0), (give_rest, 1), 16,
     ]
     for step in steps:
         if isinstance(step, int):
@@ -285,7 +380,13 @@
     def _():
         gone(state.at[:, pl.ds(0, NX - 1)], 0)
         gone(total.at[:, :, pl.ds(0, nz - 1)], 1)
-        gone(col_out.at[:, :, pl.ds(0, nz - 1)], 2)
+        gone(col_out.at[1, :, pl.ds(0, nz - 1)], 2)
+        gone(col_out.at[0, :, pl.ds(0, nz - 2)], 2)
+
+        @pl.when(z == 0)
+        def _():
+            gone(col_out.at[0, :, nz - 1], 2)
+
         gone(row_out.at[0], 3)
         gone(row_out.at[1, :, pl.ds(0, NX - 1)], 4)
 
@@ -368,7 +469,8 @@
                 vmem((2, PIECES, NX, TALL, DH), f32),
                 dma((4,)),
                 dma((5,)),
-                dma((2, PIECES)), dma((2, PIECES)), dma((2, PIECES)), dma((2, PIECES)),
+                dma((2, PIECES)), dma((2, PIECES, 2)), dma((2, PIECES)), dma((2, PIECES)),
+                pltpu.SemaphoreType.REGULAR,
             ],
             compiler_params=pltpu.CompilerParams(
                 collective_id=0, has_side_effects=True, vmem_limit_bytes=32 * 1024 * 1024

time: 33.1 us -> 30.1 us (0.909)
  Pallas kernels: 32.2 us -> 29.2 us
    pallas_call x1, Pallas kernels: 30.1 us -> 27 us  [on_device(): pl.pallas_call(functools.partial(kernel, nz, factor), out_shape=(vmem((le...]
where the time goes in v4:
time: 30.1 us; the launch traced here: 30 us
  Pallas kernels  29.2 us (97%)
  between operations  0.8 us (3%)
    pallas_call x1, Pallas kernels, on_device(): pl.pallas_call(functools.partial(kernel, nz, factor), out_shape=(vmem((le...  27 us
    pallas_call x1, Pallas kernels, on_device(): pl.pallas_call(functools.partial(last_part, factor), out_shape=(out,) * 4...  2.17 us

profile of v4, /device:TPU:1, one launch (start us, length us, event | category | flops | bytes accessed | tf_op | source)
XLA Modules:
  0.0 30.0 jit_solution(15620413646123213057)
XLA Ops:
  0.6 27.0 %linear_attention.1 = (bf16[1024,512]{1,0:T(8,128)(2,1)S(1)}, bf16[1024,512]{1,0:T(8,128)(2,1)S(1)}, f32[1024,512]{1,0:T(8,128)S(1)}, f32[1024,512]{1,0:T(8,128)...) custom-call(bf16[1024,512]{1,0:T(8,128)(2,1)} %q_hbm.1, ...), custom_call_target="tpu_custom_call" | custom-call | tf_op jit(solution)/shard_map/linear_attention/pallas_call | solution.py:444
  27.6 2.2 %last_part.1 = (bf16[1024,512]{1,0:T(8,128)(2,1)}, bf16[1024,512]{1,0:T(8,128)(2,1)}, bf16[1024,512]{1,0:T(8,128)(2,1)}, bf16[1024,512]{1,0:T(8,128)(2,1)}) custom-call(bf16[1024,512]{1,0:T(8,128)(2,1)S(1)} %get-tuple-element.11.att, bf16[1024,512]{1,0:T(8,128)(2,1)S(1)} %get-tuple-element.12.gq, f32[1024,512]{1,0:T(8,128)S(1)} %get-tuple-element.13.acc_k, ...), custom_call_target="tpu_custom_call" | custom-call | tf_op jit(solution)/shard_map/last_part/pallas_call | solution.py:484

commit v5 on v4

--- a/solution.py
+++ b/solution.py
@@ -40,11 +40,20 @@
     return upper, lower
 
 
+def inter_last(factor, out, acc, left, hi, lo, across, c, parts):
+    both = jnp.concatenate([hi, lo], axis=1 if across else 0)
+    for r in parts:
+        own = pl.ds(r * BLK, BLK)
+        lhs = left[own, c]
+        lhs = jnp.concatenate([lhs, lhs], axis=1)
+        inter = inner_last(lhs, both) if across else plain(lhs, both)
+        out[own, c] = (factor * (acc[own, c] + inter)).astype(jnp.bfloat16)
+
+
 def kernel(
     nz, factor,
     q_hbm, k_hbm, v_hbm, g_hbm,
-    att, gq, acc_k, acc_v, k, v, suffix,
-    q, g, acc_a, acc_q,
+    done_a, done_b, acc_a, acc_q, acc_k, acc_v, q, k, v, g, open_state,
     state, row_in, row_out, total, col_in, col_out, column, entering,
     in_sem, sent, got1, got2, got3, got4, ready,
 ):
@@ -77,19 +86,32 @@
 
     early = z < FEW
 
-    def load(n):
-        src, dst = ((k_hbm, k), (v_hbm, v), (q_hbm, q), (g_hbm, g))[n]
-        return pltpu.make_async_copy(src, dst, in_sem.at[n])
+    ORDER = (1, 3, 2, 0)
+    pairs = ((k_hbm, k), (v_hbm, v), (q_hbm, q), (g_hbm, g))
+
+    def load_all(n):
+        src, dst = pairs[n]
+        return pltpu.make_async_copy(src, dst, in_sem.at[n % 2, NX])
+
+    def load_head(n, i):
+        src, dst = pairs[n]
+        c = cols(along_x(i))
+        return pltpu.make_async_copy(src.at[:, c], dst.at[:, c], in_sem.at[n % 2, i])
+
+    def load(first, second):
+        for i in ORDER:
+            for n in first:
+                load_head(n, i).start()
+        for n in second:
+            load_all(n).start()
 
     @pl.when(early)
     def _():
-        for n in (0, 1, 2, 3):
-            load(n).start()
+        load((0, 1), (2, 3))
 
     @pl.when(jnp.logical_not(early))
     def _():
-        for n in (2, 3, 0, 1):
-            load(n).start()
+        load((2, 3), (0, 1))
 
     barrier = pltpu.get_barrier_semaphore()
 
@@ -114,8 +136,6 @@
     def arrived(ref, sem):
         pltpu.make_async_copy(ref, ref, sem).wait()
 
-    ORDER = (1, 3, 2, 0)
-
     def hand_in(st, part, i):
         send(
             state.at[st, i, rows(part)], row_in.at[st, part, core * NX + x],
@@ -133,23 +153,25 @@
 
     def states(st, first):
         left, right = ((k, v), (q, g))[st]
-        load(2 * st).wait()
-        load(2 * st + 1).wait()
+        if not first:
+            load_all(2 * st).wait()
+            load_all(2 * st + 1).wait()
         for i in ORDER:
             h = along_x(i)
+            if first:
+                load_head(2 * st, i).wait()
+                load_head(2 * st + 1, i).wait()
             state[st, i] = inner_first(left[:, cols(h)], right[:, cols(h)])
             if first:
                 if i == 1:
                     @pl.when(scans)
                     def _():
                         pl.semaphore_wait(ready, 1)
-                for part in range(PIECES):
-                    hand_in(st, part, i) if i > 0 else hand_in_own(st, part)
-        if not first:
-            for part in range(PIECES):
-                for i in ORDER[:3]:
-                    hand_in(st, part, i)
-                hand_in_own(st, part)
+                hand_in(st, 0, i) if i > 0 else hand_in_own(st, 0)
+        for part in range(1 if first else 0, PIECES):
+            for i in ORDER[:3]:
+                hand_in(st, part, i)
+            hand_in_own(st, part)
 
     def row_scan(st, part, meet=False):
         arrived(row_in.at[st, part, pl.ds(0, 2 * NX - 1)], got1.at[st, part])
@@ -300,18 +322,17 @@
             else:
                 acc[own, c] = add
 
-    def finish(h):
+    def finish(st, h):
         c = cols(h)
-        hi, lo = split(entered(0, h))
-        tall = jnp.concatenate([hi, lo], axis=0)
-        wide = jnp.concatenate([hi, lo], axis=1)
-        for out, acc, left in ((att, acc_a, q), (gq, acc_q, g)):
-            for r in range(blocks):
-                own = pl.ds(r * BLK, BLK)
-                lhs = left[own, c]
-                lhs = jnp.concatenate([lhs, lhs], axis=1)
-                inter = plain(lhs, tall) if left is q else inner_last(lhs, wide)
-                out[own, c] = (factor * (acc[own, c] + inter)).astype(jnp.bfloat16)
+        hi, lo = split(entered(st, h))
+        accs = ((acc_a, acc_q), (acc_v, acc_k))[st]
+        lefts = ((q, g), (k, v))[st]
+        for out, acc, left, across in zip((done_a, done_b), accs, lefts, (False, True)):
+            inter_last(factor, out, acc, left, hi, lo, across, c, range(blocks))
+
+    def leave(st):
+        for h in range(HEADS):
+            open_state[h, 0], open_state[h, 1] = split(entered(st, h))
 
     @pl.when(early)
     def _():
@@ -351,11 +372,24 @@
             for part in range(PIECES):
                 row_scan(0, part)
 
+    def third_scans():
+        @pl.when(early)
+        def _():
+            for part in range(PIECES):
+                give_back(1, part)
+                col_scan_rest(part)
+
+        @pl.when(jnp.logical_not(early))
+        def _():
+            for part in range(PIECES):
+                col_scan_rest(part)
+            for part in range(PIECES):
+                give_back(1, part)
+
     units = [(h, r) for h in range(HEADS) for r in range(blocks)]
     steps = [
-        6, (first_scans,), 3, (second_scans,), (col_scan, 0), (col_scan, 1), 3,
-        (give_few, 0), (give_few, 1), (col_scan_rest, 0), (col_scan_rest, 1), 1,
-        (give_back, 1, 0), (give_back, 1, 1), 2, (give_rest, 0), (give_rest, 1), 16,
+        6, (first_scans,), 1, (second_scans,), (col_scan, 0), (col_scan, 1), (give_few, 0), (give_few, 1), 4,
+        (third_scans,), (give_rest, 0), (give_rest, 1), 16,
     ]
     for step in steps:
         if isinstance(step, int):
@@ -364,14 +398,16 @@
                     unit(*units.pop(0))
         else:
             pl.when(scans)(functools.partial(*step))
-    for part in range(PIECES):
-        take(0, part)
-    for h in range(HEADS):
-        finish(h)
-    for part in range(PIECES):
-        take(1, part)
-    for h in range(HEADS):
-        suffix[h, 0], suffix[h, 1] = split(entered(1, h))
+    for near, order in ((z <= FEW, (0, 1)), (z > FEW, (1, 0))):
+        @pl.when(near)
+        def _():
+            for part in range(PIECES):
+                take(order[0], part)
+            for h in range(HEADS):
+                finish(order[0], h)
+            for part in range(PIECES):
+                take(order[1], part)
+            leave(order[1])
 
     def gone(ref, n):
         pltpu.make_async_copy(ref, ref, sent.at[n]).wait()
@@ -397,37 +433,44 @@
 
 def last_part(
     factor,
-    att, gq, acc_k, acc_v, k, v, suffix,
+    done_a, done_b, acc_a, acc_q, acc_k, acc_v, q, k, v, g, open_state,
     att_hbm, gq_hbm, gk_hbm, gv_hbm,
-    gk, gv, sem,
+    late_a, late_b, sem,
 ):
-    length = k.shape[0]
-    copies = []
-
-    def write(n, src, dst, part):
-        copy = pltpu.make_async_copy(src.at[part], dst.at[part], sem.at[n, part.start // BLK])
-        copy.start()
-        copies.append(copy)
-
-    parts = [pl.ds(r * BLK, BLK) for r in range(length // BLK)]
-    for own in parts:
-        write(0, att, att_hbm, own)
-        write(1, gq, gq_hbm, own)
-    for own in parts:
-        for h in range(HEADS):
-            c = pl.ds(h * DH, DH)
-            tall = jnp.concatenate([suffix[h, 0], suffix[h, 1]], axis=0)
-            wide = jnp.concatenate([suffix[h, 0], suffix[h, 1]], axis=1)
-            lhs = k[own, c]
-            inter = plain(jnp.concatenate([lhs, lhs], axis=1), tall)
-            gv[own, c] = (factor * (acc_v[own, c] + inter)).astype(jnp.bfloat16)
-            lhs = v[own, c]
-            inter = inner_last(jnp.concatenate([lhs, lhs], axis=1), wide)
-            gk[own, c] = (factor * (acc_k[own, c] + inter)).astype(jnp.bfloat16)
-        write(2, gk, gk_hbm, own)
-        write(3, gv, gv_hbm, own)
-    for copy in copies:
-        copy.wait()
+    blocks = k.shape[0] // BLK
+    z = lax.div(lax.axis_index("ctx"), NX)
+
+    def write(n, src, dst, r):
+        part = pl.ds(r * BLK, BLK)
+        return pltpu.make_async_copy(src.at[part], dst.at[part], sem.at[n])
+
+    def rest(first, second, accs, lefts):
+        copies = []
+        for r in range(blocks):
+            copies.append(write(0, done_a, first[0], r))
+            copies.append(write(1, done_b, first[1], r))
+        for copy in copies:
+            copy.start()
+        for r in range(blocks):
+            for h in range(HEADS):
+                c = pl.ds(h * DH, DH)
+                hi, lo = open_state[h, 0], open_state[h, 1]
+                for out, acc, left, across in zip((late_a, late_b), accs, lefts, (False, True)):
+                    inter_last(factor, out, acc, left, hi, lo, across, c, (r,))
+            for n, src in ((2, late_a), (3, late_b)):
+                copy = write(n, src, second[n - 2], r)
+                copy.start()
+                copies.append(copy)
+        for n, src in enumerate((done_a, done_b, late_a, late_b)):
+            pltpu.make_async_copy(src, src, sem.at[n]).wait()
+
+    @pl.when(z <= FEW)
+    def _():
+        rest((att_hbm, gq_hbm), (gv_hbm, gk_hbm), (acc_v, acc_k), (k, v))
+
+    @pl.when(z > FEW)
+    def _():
+        rest((gv_hbm, gk_hbm), (att_hbm, gq_hbm), (acc_a, acc_q), (q, g))
 
 
 def solution(mesh):
@@ -443,22 +486,13 @@
         vmem, hbm = pltpu.VMEM, pltpu.HBM
         ready = pl.pallas_call(
             functools.partial(kernel, nz, factor),
-            out_shape=(
-                vmem((length, width), bf16),
-                vmem((length, width), bf16),
-                vmem((length, width), f32),
-                vmem((length, width), f32),
-                vmem((length, width), bf16),
-                vmem((length, width), bf16),
-                vmem((HEADS, 2, DH, DH), bf16),
-            ),
+            out_shape=(vmem((length, width), bf16),) * 2
+            + (vmem((length, width), f32),) * 4
+            + (vmem((length, width), bf16),) * 4
+            + (vmem((HEADS, 2, DH, DH), bf16),),
             in_specs=[pl.BlockSpec(memory_space=hbm)] * 4,
-            out_specs=(pl.BlockSpec(memory_space=vmem),) * 7,
+            out_specs=(pl.BlockSpec(memory_space=vmem),) * 11,
             scratch_shapes=[
-                vmem((length, width), bf16),
-                vmem((length, width), bf16),
-                vmem((length, width), f32),
-                vmem((length, width), f32),
                 vmem((2, NX, DH, DH), f32),
                 vmem((2, PIECES, 2 * NX, TALL, DH), f32),
                 vmem((2, 2, NX, DH, DH), f32),
@@ -467,7 +501,7 @@
                 vmem((2, PIECES, nz, 2, sub, DH), f32),
                 vmem((2, PIECES, nz, 2, sub, DH), f32),
                 vmem((2, PIECES, NX, TALL, DH), f32),
-                dma((4,)),
+                dma((2, NX + 1)),
                 dma((5,)),
                 dma((2, PIECES)), dma((2, PIECES, 2)), dma((2, PIECES)), dma((2, PIECES)),
                 pltpu.SemaphoreType.REGULAR,
@@ -484,12 +518,12 @@
         return pl.pallas_call(
             functools.partial(last_part, factor),
             out_shape=(out,) * 4,
-            in_specs=[pl.BlockSpec(memory_space=vmem)] * 7,
+            in_specs=[pl.BlockSpec(memory_space=vmem)] * 11,
             out_specs=(pl.BlockSpec(memory_space=hbm),) * 4,
             scratch_shapes=[
                 vmem((length, width), bf16),
                 vmem((length, width), bf16),
-                dma((4, length // BLK)),
+                dma((4,)),
             ],
             compiler_params=pltpu.CompilerParams(vmem_limit_bytes=16 * 1024 * 1024),
             name="last_part",

time: 30.1 us -> 29.4 us (0.977)
  Pallas kernels: 29.2 us -> 28.5 us
    pallas_call x1, Pallas kernels: 27 us -> 26.5 us  [on_device(): pl.pallas_call(functools.partial(kernel, nz, factor), out_shape=(vmem((le...]
where the time goes in v5:
time: 29.4 us; the launch traced here: 29.3 us
  Pallas kernels  28.5 us (97%)
  between operations  0.8 us (3%)
    pallas_call x1, Pallas kernels, on_device(): pl.pallas_call(functools.partial(kernel, nz, factor), out_shape=(vmem((le...  26.5 us
    pallas_call x1, Pallas kernels, on_device(): pl.pallas_call(functools.partial(last_part, factor), out_shape=(out,) * 4...  2.07 us

profile of v5, /device:TPU:1, one launch (start us, length us, event | category | flops | bytes accessed | tf_op | source)
XLA Modules:
  0.0 29.3 jit_solution(5972663433167674171)
XLA Ops:
  0.6 26.5 %linear_attention.1 = (bf16[1024,512]{1,0:T(8,128)(2,1)S(1)}, bf16[1024,512]{1,0:T(8,128)(2,1)S(1)}, f32[1024,512]{1,0:T(8,128)S(1)}, f32[1024,512]{1,0:T(8,128)...) custom-call(bf16[1024,512]{1,0:T(8,128)(2,1)} %q_hbm.1, ...), custom_call_target="tpu_custom_call" | custom-call | tf_op jit(solution)/shard_map/linear_attention/pallas_call | solution.py:487
  27.1 2.1 %last_part.1 = (bf16[1024,512]{1,0:T(8,128)(2,1)}, bf16[1024,512]{1,0:T(8,128)(2,1)}, bf16[1024,512]{1,0:T(8,128)(2,1)}, bf16[1024,512]{1,0:T(8,128)(2,1)}) custom-call(bf16[1024,512]{1,0:T(8,128)(2,1)S(1)} %get-tuple-element.15.done_a, bf16[1024,512]{1,0:T(8,128)(2,1)S(1)} %get-tuple-element.16.done_b, f32[1024,512]{1,0:T(8,128)S(1)} %get-tuple-element.17.acc_a, ...), custom_call_target="tpu_custom_call" | custom-call | tf_op jit(solution)/shard_map/last_part/pallas_call | solution.py:518

commit v6 on v5

--- a/solution.py
+++ b/solution.py
@@ -388,7 +388,7 @@
 
     units = [(h, r) for h in range(HEADS) for r in range(blocks)]
     steps = [
-        6, (first_scans,), 1, (second_scans,), (col_scan, 0), (col_scan, 1), (give_few, 0), (give_few, 1), 4,
+        6, (first_scans,), (second_scans,), (col_scan, 0), (col_scan, 1), (give_few, 0), (give_few, 1), 5,
         (third_scans,), (give_rest, 0), (give_rest, 1), 16,
     ]
     for step in steps:

time: 29.4 us -> 30.1 us (1.024); the launches traced: 29.3 us -> 29.6 us
  no operation moved by 1% of the time
where the time goes in v6:
time: 30.1 us; the launch traced here: 29.6 us
  Pallas kernels  28.8 us (96%)
  between operations  0.8 us (3%)
    pallas_call x1, Pallas kernels, on_device(): pl.pallas_call(functools.partial(kernel, nz, factor), out_shape=(vmem((le...  26.8 us
    pallas_call x1, Pallas kernels, on_device(): pl.pallas_call(functools.partial(last_part, factor), out_shape=(out,) * 4...  2.07 us

profile of v6, /device:TPU:1, one launch (start us, length us, event | category | flops | bytes accessed | tf_op | source)
XLA Modules:
  0.0 29.6 jit_solution(1380246601405251719)
XLA Ops:
  0.6 26.8 %linear_attention.1 = (bf16[1024,512]{1,0:T(8,128)(2,1)S(1)}, bf16[1024,512]{1,0:T(8,128)(2,1)S(1)}, f32[1024,512]{1,0:T(8,128)S(1)}, f32[1024,512]{1,0:T(8,128)...) custom-call(bf16[1024,512]{1,0:T(8,128)(2,1)} %q_hbm.1, ...), custom_call_target="tpu_custom_call" | custom-call | tf_op jit(solution)/shard_map/linear_attention/pallas_call | solution.py:487
  27.4 2.1 %last_part.1 = (bf16[1024,512]{1,0:T(8,128)(2,1)}, bf16[1024,512]{1,0:T(8,128)(2,1)}, bf16[1024,512]{1,0:T(8,128)(2,1)}, bf16[1024,512]{1,0:T(8,128)(2,1)}) custom-call(bf16[1024,512]{1,0:T(8,128)(2,1)S(1)} %get-tuple-element.15.done_a, bf16[1024,512]{1,0:T(8,128)(2,1)S(1)} %get-tuple-element.16.done_b, f32[1024,512]{1,0:T(8,128)S(1)} %get-tuple-element.17.acc_a, ...), custom_call_target="tpu_custom_call" | custom-call | tf_op jit(solution)/shard_map/last_part/pallas_call | solution.py:518
